TPU v7x, 32 devices: a whole 2x2x4 slice. The times are simulated.
32 devices in a mesh: batch: 4 (over y, x), ctx: 8 (over z, core).
Axes of the slice: x: 2, y: 2, z: 4, core: 2. Of those that a mesh axis runs over, the one named last changes fastest.
Arguments:
- hidden: bfloat16 [4, 1024, 768], P('batch', 'ctx'), may hold values from -6 to 6
- cotangent: bfloat16 [4, 1024, 768], P('batch', 'ctx'), may hold values from -6 to 6
- w_qkv: bfloat16 [768, 2304], P(('batch', 'ctx')), may hold values from -3 to 3
- w_proj: bfloat16 [768, 768], P(('batch', 'ctx')), may hold values from -1.25 to 1.25
- w_inner: bfloat16 [768, 2304], P(('batch', 'ctx')), may hold values from -0.21875 to 0.21875
- w_down: bfloat16 [768, 1152], P(('batch', 'ctx')), may hold values from -0.1875 to 0.1875
- norm1_gain: bfloat16 [768], P(('batch', 'ctx')), may hold values from 0.5 to 1.5
- norm2_gain: bfloat16 [768], P(('batch', 'ctx')), may hold values from 0.5 to 1.5
Outputs:
- hidden_out: bfloat16 [4, 1024, 768], P('batch', 'ctx')
- hidden_grad: float32 [4, 1024, 768], P('batch', 'ctx')
- qkv_grad: float32 [768, 2304], P(('batch', 'ctx'))
- proj_grad: float32 [768, 768], P(('batch', 'ctx'))
- inner_grad: float32 [768, 2304], P(('batch', 'ctx'))
- down_grad: float32 [768, 1152], P(('batch', 'ctx'))
- norm1_grad: float32 [768], P(('batch', 'ctx'))
- norm2_grad: float32 [768], P(('batch', 'ctx'))
All inputs are finite; a program needn't handle non-finite values.
Results may differ from a plain program's by a relative error of at most 0.02.
Values may be sent and summed in bfloat16 or wider, within the bound.
A program may use at most 192 MiB of HBM per device.

v0:
```python
import functools
import math

import jax
import jax.numpy as jnp
from jax import lax
from jax.experimental import pallas as pl
from jax.experimental.pallas import tpu as pltpu
from jax.sharding import PartitionSpec as P

D = 768
HEADS = 12
HEAD_DIM = 64
FF = 1152


norm_eps = 1e-05
rope_base = 160000.0


def apply_layer_norm(values, gain_vector):
    centre = jnp.mean(values, axis=-1, keepdims=True)
    shifted = values - centre
    spread = jnp.mean(shifted * shifted, axis=-1, keepdims=True)
    inverse = lax.rsqrt(spread + norm_eps)
    normed = shifted * inverse
    return (normed * gain_vector, normed, inverse)


def layer_norm_gradient(upstream, gain_vector, normed, inverse):
    scaled = upstream * gain_vector
    first_mean = jnp.mean(scaled, axis=-1, keepdims=True)
    second_mean = jnp.mean(scaled * normed, axis=-1, keepdims=True)
    return (
        inverse * (scaled - first_mean - normed * second_mean),
        jnp.sum(upstream * normed, axis=0),
    )


def rope_tables(offset, row_count, head_width):
    half_dim = head_width // 2
    position = (offset + jnp.arange(row_count, dtype=jnp.int32)).astype(jnp.float32)
    exponent = jnp.arange(half_dim, dtype=jnp.int32).astype(jnp.float32) * (-2.0 / head_width)
    angles = position[:, None] * jnp.power(rope_base, exponent)[None, :]
    return (jnp.cos(angles), jnp.sin(angles))


def rotate(values, cosine, sine_table, direction):
    half_dim = values.shape[-1] // 2
    front_half = values[..., :half_dim]
    back_half = values[..., half_dim:]
    cos_rows = cosine[:, None, :]
    sin_rows = sine_table[:, None, :] * direction
    return jnp.concatenate(
        [
            front_half * cos_rows - back_half * sin_rows,
            back_half * cos_rows + front_half * sin_rows,
        ],
        axis=-1,
    )


def gelu_parts(act_input):
    normal_cdf = 0.5 * (1.0 + jax.scipy.special.erf(act_input * 0.7071067811865476))
    density = jnp.exp(-0.5 * act_input * act_input) * 0.3989422804014327
    return (act_input * normal_cdf, normal_cdf + act_input * density)


def as_heads(flat_rows):
    return flat_rows.reshape(flat_rows.shape[0], HEADS, HEAD_DIM)


EVERY = ("batch", "ctx")
LANES = 128


def weight_grad_kernel(bounds, *refs):
    count = len(bounds) - 1
    lefts, rights, gains_ref, out_ref = refs[:count], refs[count : 2 * count], refs[-2], refs[-1]
    step = pl.program_id(0)
    for index in range(count):

        @pl.when(jnp.logical_and(step >= bounds[index], step < bounds[index + 1]))
        def _(left=lefts[index], right=rights[index]):
            out_ref[...] = lax.dot_general(
                left[...],
                right[...],
                (((0,), (0,)), ((), ())),
                preferred_element_type=jnp.float32,
            ).astype(out_ref.dtype)

    @pl.when(step == bounds[count])
    def _():
        out_ref[:, :LANES] = gains_ref[...].astype(out_ref.dtype)


def weight_grads(pairs, gain_columns):
    rows, width = pairs[0][0].shape
    widths = [right.shape[1] for _, right in pairs]
    block = math.gcd(*widths)
    bounds = [0]
    for part in widths:
        bounds.append(bounds[-1] + part // block)

    def right_index(start, count, step):
        return (0, jnp.clip(step - start, 0, count - 1))

    whole = lambda step: (0, 0)
    total = sum(widths) + LANES
    return pl.pallas_call(
        functools.partial(weight_grad_kernel, tuple(bounds)),
        out_shape=jax.ShapeDtypeStruct((width, total), jnp.bfloat16),
        grid=(bounds[-1] + 1,),
        in_specs=[pl.BlockSpec((rows, width), whole) for _ in pairs]
        + [
            pl.BlockSpec(
                (rows, block),
                functools.partial(right_index, bounds[i], bounds[i + 1] - bounds[i]),
            )
            for i in range(len(pairs))
        ]
        + [pl.BlockSpec((width, LANES), whole)],
        out_specs=pl.BlockSpec((width, block), lambda step: (0, step)),
        cost_estimate=pl.CostEstimate(
            flops=2 * rows * width * total, bytes_accessed=2 * width * total, transcendentals=0
        ),
    )(*[left for left, _ in pairs], *[right for _, right in pairs], gain_columns)


def local(hidden, cotangent, w_qkv, w_proj, w_inner, w_down, norm1_gain, norm2_gain):
    token_rows = hidden.shape[1]
    score_scale = HEAD_DIM ** (-0.5)
    gains = jnp.pad(jnp.stack([norm1_gain, norm2_gain], axis=1), ((0, 0), (0, LANES - 2)))
    packed = lax.all_gather(
        jnp.concatenate([w_qkv, w_proj, w_inner, w_down, gains], axis=1), EVERY, axis=0, tiled=True
    )
    edges = [0]
    for part in (w_qkv, w_proj, w_inner, w_down, gains):
        edges.append(edges[-1] + part.shape[1])
    full_qkv, full_proj, full_inner, full_down, full_gains = (
        packed[:, edges[i] : edges[i + 1]] for i in range(5)
    )
    first_norm_gain = full_gains[:, 0].astype(jnp.float32)
    second_norm_gain = full_gains[:, 1].astype(jnp.float32)
    input_tokens = hidden[0].astype(jnp.float32)
    first_normed_rows, first_centered_rows, first_inverse_deviation = apply_layer_norm(
        input_tokens, first_norm_gain
    )
    h_one = first_normed_rows.astype(jnp.bfloat16)
    projected = jnp.dot(h_one, full_qkv, preferred_element_type=jnp.float32)
    cosine, sine_table = rope_tables(lax.axis_index("ctx") * token_rows, token_rows, HEAD_DIM)
    query_rot = rotate(as_heads(projected[:, :D]), cosine, sine_table, 1.0).astype(jnp.bfloat16)
    key_flat = (
        rotate(as_heads(projected[:, D : 2 * D]), cosine, sine_table, 1.0)
        .astype(jnp.bfloat16)
        .reshape(token_rows, D)
    )
    value_flat = projected[:, 2 * D :].astype(jnp.bfloat16)
    key_value = lax.all_gather(
        jnp.concatenate([key_flat, value_flat], axis=1), "ctx", axis=0, tiled=True
    )
    key_whole = as_heads(key_value[:, :D])
    value_whole = as_heads(key_value[:, D:])
    scores = (
        jnp.einsum("qhd,khd->hqk", query_rot, key_whole, preferred_element_type=jnp.float32)
        * score_scale
    )
    row_peak = jnp.max(scores, axis=-1)
    weights = jnp.exp(scores - row_peak[..., None])
    row_total = jnp.sum(weights, axis=-1)
    mixture = jnp.einsum(
        "hqk,khd->qhd",
        weights.astype(jnp.bfloat16),
        value_whole,
        preferred_element_type=jnp.float32,
    )
    attended = (
        (mixture / jnp.transpose(row_total)[:, :, None])
        .reshape(token_rows, D)
        .astype(jnp.bfloat16)
    )
    residual_stream = input_tokens + jnp.dot(
        attended, full_proj, preferred_element_type=jnp.float32
    )
    second_normed_rows, second_centered_rows, second_inverse_deviation = apply_layer_norm(
        residual_stream, second_norm_gain
    )
    h_two = second_normed_rows.astype(jnp.bfloat16)
    inner_all = jnp.dot(h_two, full_inner, preferred_element_type=jnp.float32)
    act_half = inner_all[:, :FF]
    gate_half = inner_all[:, FF:]
    activated, gelu_slope = gelu_parts(act_half)
    middle = (activated * gate_half).astype(jnp.bfloat16)
    output_rows = residual_stream + jnp.einsum(
        "tf,df->td", middle, full_down, preferred_element_type=jnp.float32
    )
    upstream = cotangent[0]
    d_middle = jnp.dot(upstream, full_down, preferred_element_type=jnp.float32)
    d_inner = jnp.concatenate(
        [d_middle * gate_half * gelu_slope, d_middle * activated], axis=-1
    ).astype(jnp.bfloat16)
    second_hidden_gradient = jnp.einsum(
        "te,de->td", d_inner, full_inner, preferred_element_type=jnp.float32
    )
    residual_norm_gradient, second_gain_portion = layer_norm_gradient(
        second_hidden_gradient, second_norm_gain, second_centered_rows, second_inverse_deviation
    )
    d_resid = upstream.astype(jnp.float32) + residual_norm_gradient
    d_resid_low = d_resid.astype(jnp.bfloat16)
    d_attended = jnp.einsum(
        "td,ed->te", d_resid_low, full_proj, preferred_element_type=jnp.float32
    ).astype(jnp.bfloat16)
    grad_heads = as_heads(d_attended)
    row_delta = jnp.transpose(
        jnp.sum(grad_heads.astype(jnp.float32) * as_heads(attended).astype(jnp.float32), axis=-1)
    )
    probabilities = weights * (1.0 / row_total)[..., None]
    grad_dots = jnp.einsum(
        "qhd,khd->hqk", grad_heads, value_whole, preferred_element_type=jnp.float32
    )
    dscore = (probabilities * (grad_dots - row_delta[..., None])).astype(jnp.bfloat16)
    probs_low = probabilities.astype(jnp.bfloat16)
    key_terms = (
        jnp.einsum("hqk,qhd->khd", dscore, query_rot, preferred_element_type=jnp.float32)
        * score_scale
    )
    value_terms = jnp.einsum(
        "hqk,qhd->khd", probs_low, grad_heads, preferred_element_type=jnp.float32
    )
    whole_rows = key_value.shape[0]
    key_value_sum = lax.psum_scatter(
        jnp.concatenate(
            [
                key_terms.reshape(whole_rows, D).astype(jnp.bfloat16),
                value_terms.reshape(whole_rows, D).astype(jnp.bfloat16),
            ],
            axis=1,
        ),
        "ctx",
        scatter_dimension=0,
        tiled=True,
    )
    query_grad = (
        jnp.einsum("hqk,khd->qhd", dscore, key_whole, preferred_element_type=jnp.float32)
        * score_scale
    )
    d_query = rotate(query_grad, cosine, sine_table, -1.0)
    d_key = rotate(as_heads(key_value_sum[:, :D].astype(jnp.float32)), cosine, sine_table, -1.0)
    d_projected = jnp.concatenate(
        [
            d_query.reshape(token_rows, D).astype(jnp.bfloat16),
            d_key.reshape(token_rows, D).astype(jnp.bfloat16),
            key_value_sum[:, D:],
        ],
        axis=-1,
    )
    first_hidden_gradient = jnp.einsum(
        "te,de->td", d_projected, full_qkv, preferred_element_type=jnp.float32
    )
    input_norm_gradient, first_gain_portion = layer_norm_gradient(
        first_hidden_gradient, first_norm_gain, first_centered_rows, first_inverse_deviation
    )
    input_grad = d_resid + input_norm_gradient
    gain_columns = jnp.pad(
        jnp.stack([first_gain_portion, second_gain_portion], axis=1), ((0, 0), (0, LANES - 2))
    )
    grad_terms = weight_grads(
        [(h_one, d_projected), (attended, d_resid_low), (h_two, d_inner), (upstream, middle)],
        gain_columns,
    )
    grad_share = lax.psum_scatter(
        grad_terms, EVERY, scatter_dimension=0, tiled=True
    ).astype(jnp.float32)
    return (
        output_rows.astype(jnp.bfloat16)[None],
        input_grad[None],
        grad_share[:, edges[0] : edges[1]],
        grad_share[:, edges[1] : edges[2]],
        grad_share[:, edges[2] : edges[3]],
        grad_share[:, edges[3] : edges[4]],
        grad_share[:, edges[4]],
        grad_share[:, edges[4] + 1],
    )


def solution(mesh):
    placed = (
        P("batch", "ctx", None),
        P("batch", "ctx", None),
        P(("batch", "ctx"), None),
        P(("batch", "ctx"), None),
        P(("batch", "ctx"), None),
        P(("batch", "ctx"), None),
        P(("batch", "ctx")),
        P(("batch", "ctx")),
    )
    return jax.shard_map(
        local,
        mesh=mesh,
        in_specs=placed,
        out_specs=(
            P("batch", "ctx", None),
            P("batch", "ctx", None),
            P(("batch", "ctx"), None),
            P(("batch", "ctx"), None),
            P(("batch", "ctx"), None),
            P(("batch", "ctx"), None),
            P(("batch", "ctx")),
            P(("batch", "ctx")),
        ),
        check_vma=False,
    )
```

profile of v0, /device:TPU:0, one launch (start us, length us, event | category | flops | bytes accessed | tf_op | source)
XLA Modules:
  0.0 392.9 jit_solution(6042153293724463607)
XLA Ops:
  12.2 1.0 convert_reduce_fusion
  13.3 1.1 fusion.58
  15.2 84.9 %all-gather.3.cloned.1.call-done = bf16[768,6656]{1,0:T(8,128)(2,1)} async-done(((bf16[24,6656]{1,0:T(8,128)(2,1)}), bf16[768,6656]{1,0:T(8,128)(2,1)}) %all-gather.3.cloned.1.call-update) | async-done | bytes 10223632 | tf_op jit(solution)/shard_map/all_gather | solution.py:134
  100.1 1.9 convert_reduce_fusion.1
  102.0 1.1 fusion.51.refs_0_
  103.1 2.7 fusion.10
  107.5 36.9 %all-gather.5.cloned.1.call-done = bf16[1024,1536]{1,0:T(8,128)(2,1)} async-done(((bf16[128,1536]{1,0:T(8,128)(2,1)}), bf16[1024,1536]{1,0:T(8,128)(2,1)}) %all-gather.5.cloned.1.call-update) | async-done | bytes 3145744 | tf_op jit(solution)/shard_map/all_gather | solution.py:159
  144.4 3.2 fusion.66
  148.4 2.3 copy.54
  150.7 1.1 multiply_reduce_fusion
  151.8 1.3 fusion.12
  153.2 1.9 copy-done
  155.0 1.4 fusion.33
  159.1 1.4 fusion.43
  160.5 1.9 multiply_reduce_fusion.1
  164.1 5.8 %fusion.13 = bf16[12,64,1024]{2,1,0:T(8,128)(2,1)} fusion(bf16[128,12,64]{0,2,1:T(8,128)(2,1)S(1)} %bitcast.99, f32[12,128]{1,0:T(8,128)S(1)} %broadcast_divide_fusion, f32[12,128]{1,0:T(8,128)S(1)} %copy-done.26, f32[12,128,1024]{2,1,0:T(8,128)} %copy-done), kind=kOutput, calls=%fused_computation.20 | convolution fusion | flops 208404480 | bytes 8073216 | tf_op jit(solution)/shard_map/hqk,qhd->khd/dot_general | solution.py:227
  170.0 2.4 multiply_convert_fusion
  172.3 1.6 copy-done.1
  175.3 1.7 copy.60
  177.0 2.0 pad_maximum_fusion
  179.2 1.9 copy.65.refs_1_
  181.1 1.3 stack.22
  182.5 3.4 fusion.23
  186.7 31.7 %reduce-scatter.3.cloned.1.call-done = bf16[128,1536]{1,0:T(8,128)(2,1)} async-done(((bf16[1024,1536]{1,0:T(8,128)(2,1)}), bf16[128,1536]{1,0:T(8,128)(2,1)}) %reduce-scatter.3.cloned.1.call-update) | async-done | bytes 393232 | tf_op jit(solution)/shard_map/reduce_scatter | solution.py:231
  218.4 1.1 slice_convert_fusion.1
  221.7 3.4 fusion.57
  226.2 14.5 %shard_map.143 = bf16[768,6656]{1,0:T(8,128)(2,1)} custom-call(bf16[128,768]{1,0:T(8,128)(2,1)} %copy-done.8, bf16[128,768]{1,0:T(8,128)(2,1)} %copy.65.refs_1_, bf16[128,768]{1,0:T(8,128)(2,1)} %copy-done.9, bf16[128,768]{1,0:T(8,128)(2,1)} %bitcast.109, bf16[128,2304]{1,0:T(8,128)(2,1)} %pad_maximum_fusion.2.refs_4_, bf16[128,768]{1,0:T(8,128)(2,1)} %copy-done.18, ...), custom_call_target="tpu_custom_call" | custom-call | flops 1308622848 | bytes 10223616 | tf_op jit(solution)/shard_map/pallas_call | solution.py:110
  241.6 2.8 fusion.27
  245.4 134.7 %reduce-scatter.5.cloned.1.call-done = bf16[24,6656]{1,0:T(8,128)(2,1)} async-done(((bf16[768,6656]{1,0:T(8,128)(2,1)}), bf16[24,6656]{1,0:T(8,128)(2,1)}) %reduce-scatter.5.cloned.1.call-update) | async-done | bytes 319504 | tf_op jit(solution)/shard_map/reduce_scatter | solution.py:271
  381.7 1.4 slice.144
  383.1 1.5 slice.146
  384.6 1.7 fusion.68
  (140 shorter events, 21.6 us)
Async XLA Ops:
  7.2 92.9 %all-gather.3.cloned.1.call-start = ((), (), s32[]{:S(2)}) async-start(), calls=%async_computation.2 | async-start | bytes 10543104 | tf_op jit(solution)/shard_map/all_gather | solution.py:134
  12.2 132.2 %all-gather.5.cloned.1.call-start = ((), (), s32[]{:S(2)}) async-start(), calls=%async_computation.3 | async-start | bytes 3538944 | tf_op jit(solution)/shard_map/all_gather | solution.py:159
  13.3 92.6 %copy-start.31 = (f32[128]{0:T(128)}, f32[128]{0:T(128)S(1)}, u32[]{:S(2)}) copy-start(f32[128]{0:T(128)S(1)} %broadcast_multiply_fusion.6) | copy-start | bytes 1540
  14.4 91.5 %copy-start.33 = (f32[128]{0:T(128)}, f32[128]{0:T(128)S(1)}, u32[]{:S(2)}) copy-start(f32[128]{0:T(128)S(1)} %add_rsqrt_fusion.1) | copy-start | bytes 1540
  102.0 4.0 %copy-start.27 = (f32[768]{0:T(1024)}, f32[768]{0:T(1024)S(1)}, u32[]{:S(2)}) copy-start(f32[768]{0:T(1024)S(1)} %get-tuple-element.9) | copy-start | bytes 9220
  106.4 44.2 %copy-start.13 = (bf16[128,12,32]{0,2,1:T(8,128)(2,1)}, bf16[128,12,32]{0,2,1:T(8,128)(2,1)S(1)}, u32[]{:S(2)}) copy-start(bf16[128,12,32]{0,2,1:T(8,128)(2,1)S(1)} %get-tuple-element.31) | copy-start | bytes 294916
  106.4 44.2 %copy-start.15 = (bf16[128,12,32]{0,2,1:T(8,128)(2,1)}, bf16[128,12,32]{0,2,1:T(8,128)(2,1)S(1)}, u32[]{:S(2)}) copy-start(bf16[128,12,32]{0,2,1:T(8,128)(2,1)S(1)} %get-tuple-element.32) | copy-start | bytes 294916
  107.4 111.0 %reduce-scatter.3.cloned.1.call-start = ((), (), s32[]{:S(2)}) async-start(), calls=%async_computation.4 | async-start | bytes 3538944 | tf_op jit(solution)/shard_map/reduce_scatter | solution.py:231
  148.3 3.5 copy-start.3
  150.7 5.8 %slice-start.2 = ((s8[10223616]{0:T(1024)(128)(4,1)}), s8[4194304]{0:T(1024)(128)(4,1)S(1)}, s32[]{:S(2)}) async-start(s8[10223616]{0:T(1024)(128)(4,1)} %bitcast.92), calls=%async_computation.8 | async-start | bytes 8388608
  150.7 6.3 %slice-start.3 = ((s8[10223616]{0:T(1024)(128)(4,1)}), s8[4194304]{0:T(1024)(128)(4,1)S(1)}, s32[]{:S(2)}) async-start(s8[10223616]{0:T(1024)(128)(4,1)} %bitcast.92), calls=%async_computation.9 | async-start | bytes 8388608
  151.8 3.2 copy-start
  151.8 3.2 copy-start.25
  155.0 3.2 copy-start.29
  156.4 7.6 %copy-start.10 = (bf16[128,12,64]{0,2,1:T(8,128)(2,1)}, bf16[128,12,64]{0,2,1:T(8,128)(2,1)S(1)}, u32[]{:S(2)}) copy-start(bf16[128,12,64]{0,2,1:T(8,128)(2,1)S(1)} %fusion.33) | copy-start | bytes 589828
  162.4 7.5 %slice-start = ((s8[6291456]{0:T(1024)(128)(4,1)}), s8[2097152]{0:T(1024)(128)(4,1)S(1)}, s32[]{:S(2)}) async-start(s8[6291456]{0:T(1024)(128)(4,1)} %bitcast.88), calls=%async_computation.6 | async-start | bytes 4194304
  163.3 6.6 %copy-start.18 = (bf16[128,768]{1,0:T(8,128)(2,1)}, bf16[128,768]{1,0:T(8,128)(2,1)S(1)}, u32[]{:S(2)}) copy-start(bf16[128,768]{1,0:T(8,128)(2,1)S(1)} %get-tuple-element.18.refs_5_) | copy-start | bytes 589828
  164.1 5.8 %slice-start.1 = ((s8[6291456]{0:T(1024)(128)(4,1)}), s8[4194304]{0:T(1024)(128)(4,1)S(1)}, s32[]{:S(2)}) async-start(s8[6291456]{0:T(1024)(128)(4,1)} %bitcast.88), calls=%async_computation.7 | async-start | bytes 8388608
  164.1 5.8 %copy-start.5 = (bf16[1024,768]{0,1:T(8,128)(2,1)S(1)}, bf16[1024,768]{0,1:T(8,128)(2,1)}, u32[]{:S(2)}) copy-start(bf16[1024,768]{0,1:T(8,128)(2,1)} %copy-done.4) | copy-start | bytes 4718596
  169.9 4.0 %copy-start.14 = (bf16[128,12,32]{0,2,1:T(8,128)(2,1)S(1)}, bf16[128,12,32]{0,2,1:T(8,128)(2,1)}, u32[]{:S(2)}) copy-start(bf16[128,12,32]{0,2,1:T(8,128)(2,1)} %copy-done.13) | copy-start | bytes 294916
  169.9 4.0 %copy-start.16 = (bf16[128,12,32]{0,2,1:T(8,128)(2,1)S(1)}, bf16[128,12,32]{0,2,1:T(8,128)(2,1)}, u32[]{:S(2)}) copy-start(bf16[128,12,32]{0,2,1:T(8,128)(2,1)} %copy-done.15) | copy-start | bytes 294916
  179.0 3.5 copy-start.2
  179.0 201.0 %reduce-scatter.5.cloned.1.call-start = ((), (), s32[]{:S(2)}) async-start(), calls=%async_computation.5 | async-start | bytes 10543104 | tf_op jit(solution)/shard_map/reduce_scatter | solution.py:271
  181.1 4.7 %copy-start.22 = (bf16[128,1152]{1,0:T(8,128)(2,1)S(1)}, bf16[128,1152]{1,0:T(8,128)(2,1)}, u32[]{:S(2)}) copy-start(bf16[128,1152]{1,0:T(8,128)(2,1)} %copy-done.21) | copy-start | bytes 884740
  181.1 4.7 %copy-start.24 = (bf16[128,1152]{1,0:T(8,128)(2,1)S(1)}, bf16[128,1152]{1,0:T(8,128)(2,1)}, u32[]{:S(2)}) copy-start(bf16[128,1152]{1,0:T(8,128)(2,1)} %copy-done.23) | copy-start | bytes 884740
  185.8 33.8 %copy-start.11 = (f32[128,12,64]{0,2,1:T(8,128)S(1)}, f32[128,12,64]{0,2,1:T(8,128)}, u32[]{:S(2)}) copy-start(f32[128,12,64]{0,2,1:T(8,128)} %fusion.23) | copy-start | bytes 1179652
  186.7 35.0 %copy-start.7 = (bf16[1,128,768]{2,1,0:T(8,128)(2,1)S(1)}, bf16[1,128,768]{2,1,0:T(8,128)(2,1)}, u32[]{:S(2)}) copy-start(bf16[1,128,768]{2,1,0:T(8,128)(2,1)} %param.8) | copy-start | bytes 589828
  186.7 35.0 %copy-start.28 = (f32[768]{0:T(1024)S(1)}, f32[768]{0:T(1024)}, u32[]{:S(2)}) copy-start(f32[768]{0:T(1024)} %copy-done.27) | copy-start | bytes 9220
  186.7 35.0 %copy-start.32 = (f32[128]{0:T(128)S(1)}, f32[128]{0:T(128)}, u32[]{:S(2)}) copy-start(f32[128]{0:T(128)} %copy-done.31) | copy-start | bytes 1540
  186.7 35.0 %copy-start.34 = (f32[128]{0:T(128)S(1)}, f32[128]{0:T(128)}, u32[]{:S(2)}) copy-start(f32[128]{0:T(128)} %copy-done.33) | copy-start | bytes 1540
  221.7 3.4 copy-start.30
  240.7 3.8 copy-start.12
  (12 other events, 22.5 us)
Sparse Core Ops, SparseCore 0:
  12.3 87.7 all-gather.2
  107.5 36.7 all-gather.4
  179.1 39.2 reduce-scatter.2
  240.8 139.1 reduce-scatter.4
where the time goes:
time: 394 us; the launch traced here: 393 us
  waiting for transfers between devices  288 us (73%)
  local copies, waits for them, and re-layouts  29.3 us (7%)
  matrix products  28.4 us (7%)
  other arithmetic  17.7 us (4%)
  Pallas kernels  14.5 us (4%)
  between operations  14.4 us (4%)
    reduce_scatter x1, waiting for transfers between devices, local(): lax.psum_scatter(grad_terms, EVERY, scatter_dimension=0, tiled=True)  135 us
    all_gather x1, waiting for transfers between devices, local(): lax.all_gather(jnp.concatenate([w_qkv, w_proj, w_inner, w_down, gains], a...  84.9 us
    all_gather x1, waiting for transfers between devices, local(): lax.all_gather(jnp.concatenate([key_flat, value_flat], axis=1), 'ctx', ax...  36.9 us
    reduce_scatter x1, waiting for transfers between devices, local(): lax.psum_scatter(jnp.concatenate([key_terms.reshape(whole_rows, D).astype...  31.7 us
    pallas_call x1, Pallas kernels, weight_grads(): pl.pallas_call(functools.partial(weight_grad_kernel, tuple(bounds)), out_...  14.5 us
    unnamed x85, local copies, waits for them, and re-layouts  9.97 us
  transfers between devices with their start and end apart: 4, of which 4 were waited for; matrix products, arithmetic and copies ran while one was open for 4% of the time, Pallas kernels for 0%

commit v1 on v0

--- a/solution.py
+++ b/solution.py
@@ -283,6 +283,939 @@
     )
 
 
+MESH = pl.DeviceIdType.MESH
+LANES = 128
+TYPE = 256
+F32 = jnp.float32
+BF16 = jnp.bfloat16
+
+
+def place():
+    b = lax.axis_index("batch")
+    t = lax.axis_index("ctx")
+    return b, t // 2, t % 2
+
+
+def plane_x(b):
+    return b + 1 - 2 * (b % 2)
+
+
+def plane_y(b):
+    return b + 2 - 4 * (b // 2)
+
+
+def remote(src, dst, send_sem, recv_sem, b, t):
+    return pltpu.make_async_remote_copy(
+        src_ref=src,
+        dst_ref=dst,
+        send_sem=send_sem,
+        recv_sem=recv_sem,
+        device_id=(b, t),
+        device_id_type=MESH,
+    )
+
+
+def greet(partners):
+    barrier = pltpu.get_barrier_semaphore()
+    for b, t in partners:
+        pl.semaphore_signal(barrier, inc=1, device_id=(b, t), device_id_type=MESH)
+    pl.semaphore_wait(barrier, len(partners))
+
+
+class Sends:
+    def __init__(self, sems):
+        self.sems, self.count, self.open = sems, 0, []
+
+    def go(self, src, dst, recv_sem, b, t, cond=None):
+        copy = remote(src, dst, self.sems.at[self.count], recv_sem, b, t)
+        self.count += 1
+        self.open.append((copy, cond))
+        if cond is None:
+            copy.start()
+        else:
+            pl.when(cond)(copy.start)
+
+    def drain(self):
+        for copy, cond in self.open:
+            if cond is None:
+                copy.wait_send()
+            else:
+                pl.when(cond)(copy.wait_send)
+        self.open = []
+
+
+def both(*conds):
+    conds = [c for c in conds if c is not None]
+    if not conds:
+        return None
+    out = conds[0]
+    for c in conds[1:]:
+        out = jnp.logical_and(out, c)
+    return out
+
+
+def front_kernel(
+    depth,
+    tokens,
+    heads,
+    hidden_ref,
+    wq_ref,
+    rest_ref,
+    rest_all,
+    att_ref,
+    q_ref,
+    k_ref,
+    v_ref,
+    o_ref,
+    lse_ref,
+    h1_ref,
+    wq_out,
+    gain_out,
+    hid_all,
+    wq_all,
+    att_own,
+    cos_ref,
+    sin_ref,
+    send_sems,
+    hid_sems,
+    wq_sems,
+    rest_sems,
+    half_sems,
+    att_sems,
+    own_sems,
+):
+    b, z, c = place()
+    t = 2 * z + c
+    bx, by = plane_x(b), plane_y(b)
+    bd = plane_x(by)
+    shard = lambda bb, zz, cc: (bb * depth + zz) * 2 + cc
+    mine = shard(b, z, c)
+    sib = (b, 2 * z + 1 - c)
+    partners = [(b, 2 * ((z + k) % depth) + c) for k in range(1, depth)]
+    partners += [(bx, t), (by, t), sib]
+    greet(partners)
+    sends = Sends(send_sems)
+    left_ok, right_ok = z > 0, z < depth - 1
+    left, right = (b, t - 2), (b, t + 2)
+
+    def arrive(dst, sem, cond=None):
+        copy = remote(dst, dst, send_sems.at[0], sem, *sib)
+        if cond is None:
+            copy.wait_recv()
+        else:
+            pl.when(cond)(copy.wait_recv)
+
+    def hid(slot):
+        return hid_all.at[slot]
+
+    def hid_start():
+        for dst, cond in ((left, left_ok), (right, right_ok), (sib, None)):
+            sends.go(hidden_ref, hid(t), hid_sems.at[t], *dst, cond=cond)
+        pltpu.make_async_copy(hidden_ref, hid(t), own_sems.at[0]).start()
+
+    def hid_step(k):
+        lo, hi = z >= k, z < depth - k
+        src = t - 2 * k
+        src_lo = jnp.maximum(src, 0)
+        arrive(hid(src_lo), hid_sems.at[src_lo], lo)
+        if k < depth - 1:
+            sends.go(hid(src_lo), hid(src_lo), hid_sems.at[src_lo], *right, cond=both(lo, right_ok))
+        sends.go(hid(src_lo), hid(src_lo), hid_sems.at[src_lo], *sib, cond=lo)
+        src_hi = jnp.minimum(t + 2 * k, 2 * depth - 1)
+        arrive(hid(src_hi), hid_sems.at[src_hi], hi)
+        if k < depth - 1:
+            sends.go(hid(src_hi), hid(src_hi), hid_sems.at[src_hi], *left, cond=both(hi, left_ok))
+        sends.go(hid(src_hi), hid(src_hi), hid_sems.at[src_hi], *sib, cond=hi)
+
+    def wq_start():
+        for k in range(1, depth):
+            zz = (z + k) % depth
+            sends.go(wq_ref.at[zz], wq_all.at[mine], wq_sems.at[mine], b, 2 * zz + c)
+        pltpu.make_async_copy(wq_ref.at[z], wq_all.at[mine], own_sems.at[1]).start()
+        for dst in ((bx, t), (by, t), sib):
+            sends.go(wq_ref.at[z], wq_all.at[mine], wq_sems.at[mine], *dst)
+
+    def wq_pass(i, targets):
+        for dst in targets:
+            sends.go(wq_all.at[i], wq_all.at[i], wq_sems.at[i], *dst)
+
+    def wq_z():
+        for k in range(1, depth):
+            i = shard(b, (z + k) % depth, c)
+            arrive(wq_all.at[i], wq_sems.at[i])
+            wq_pass(i, ((bx, t), (by, t), sib))
+
+    def wq_plane():
+        for k in range(depth):
+            zz = (z + k) % depth
+            low = zz < depth // 2
+            i = shard(bx, zz, c)
+            arrive(wq_all.at[i], wq_sems.at[i])
+            sends.go(wq_all.at[i], wq_all.at[i], wq_sems.at[i], by, t, cond=low)
+            wq_pass(i, (sib,))
+            i = shard(by, zz, c)
+            arrive(wq_all.at[i], wq_sems.at[i])
+            sends.go(
+                wq_all.at[i], wq_all.at[i], wq_sems.at[i], bx, t, cond=jnp.logical_not(low)
+            )
+            wq_pass(i, (sib,))
+
+    def wq_diag():
+        for k in range(depth):
+            i = shard(bd, (z + k) % depth, c)
+            arrive(wq_all.at[i], wq_sems.at[i])
+            wq_pass(i, (sib,))
+
+    def wq_sib():
+        for bb in range(4):
+            for zz in range(depth):
+                i = shard(bb, zz, 1 - c)
+                arrive(wq_all.at[i], wq_sems.at[i])
+
+    width = rest_ref.shape[1]
+    cut = width // 2 // LANES * LANES
+    part_a, part_b = pl.ds(0, cut), pl.ds(cut, width - cut)
+
+    def rest(i):
+        return rest_all.at[i]
+
+    def rest_start():
+        for dst, cond in (((bx, t), None), ((by, t), None), (left, left_ok), (right, right_ok), (sib, None)):
+            sends.go(rest_ref, rest(mine), rest_sems.at[mine], *dst, cond=cond)
+        pltpu.make_async_copy(rest_ref, rest(mine), own_sems.at[2]).start()
+
+    def rest_z(k, side):
+        cond = (z >= k) if side < 0 else (z < depth - k)
+        zz = jnp.clip(z + side * k, 0, depth - 1)
+        onward, on_ok = (right, right_ok) if side < 0 else (left, left_ok)
+        i = shard(b, zz, c)
+        arrive(rest(i), rest_sems.at[i], cond)
+        if k < depth - 1:
+            sends.go(rest(i), rest(i), rest_sems.at[i], *onward, cond=both(cond, on_ok))
+        for dst in ((bx, t), (by, t), sib):
+            sends.go(rest(i), rest(i), rest_sems.at[i], *dst, cond=cond)
+
+    def slot(k, side):
+        cond = None if k == 0 else ((z >= k) if side < 0 else (z < depth - k))
+        return cond, (z if k == 0 else jnp.clip(z + side * k, 0, depth - 1))
+
+    def rest_plane(k, side):
+        cond, zz = slot(k, side)
+        i = shard(bx, zz, c)
+        arrive(rest(i), rest_sems.at[i], cond)
+        sends.go(rest(i).at[:, part_a], rest(i).at[:, part_a], half_sems.at[0, i], by, t, cond=cond)
+        sends.go(rest(i), rest(i), rest_sems.at[i], *sib, cond=cond)
+        i = shard(by, zz, c)
+        arrive(rest(i), rest_sems.at[i], cond)
+        sends.go(rest(i).at[:, part_b], rest(i).at[:, part_b], half_sems.at[1, i], bx, t, cond=cond)
+        sends.go(rest(i), rest(i), rest_sems.at[i], *sib, cond=cond)
+
+    def rest_diag(k, side):
+        cond, zz = slot(k, side)
+        i = shard(bd, zz, c)
+        arrive(rest(i).at[:, part_a], half_sems.at[0, i], cond)
+        arrive(rest(i).at[:, part_b], half_sems.at[1, i], cond)
+        sends.go(rest(i), rest(i), rest_sems.at[i], *sib, cond=cond)
+
+    def rest_sib():
+        for bb in range(4):
+            for zz in range(depth):
+                i = shard(bb, zz, 1 - c)
+                arrive(rest(i), rest_sems.at[i])
+
+    order = [(0, 0)] + [(k, s) for k in range(1, depth) for s in (-1, 1)]
+    steps = []
+    for n in range(len(order) + 2):
+        if 0 < n < len(order):
+            steps.append(functools.partial(rest_z, *order[n]))
+        if 0 <= n - 1 < len(order):
+            steps.append(functools.partial(rest_plane, *order[n - 1]))
+        if 0 <= n - 2 < len(order):
+            steps.append(functools.partial(rest_diag, *order[n - 2]))
+
+    def advance(count):
+        for _ in range(min(count, len(steps))):
+            steps.pop(0)()
+
+    hid_start()
+    wq_start()
+    rest_start()
+
+    half = HEAD_DIM // 2
+    lane = lax.broadcasted_iota(jnp.int32, (tokens, LANES), 1) % half
+    freq = jnp.exp(lane.astype(F32) * (-2.0 / HEAD_DIM * math.log(rope_base)))
+    row = lax.broadcasted_iota(jnp.int32, (tokens, LANES), 0).astype(F32)
+    cos_ref[...] = jnp.cos(row * freq)
+    sin_ref[...] = jnp.sin(row * freq)
+
+    wq_z()
+    hid_step(1)
+    wq_plane()
+    hid_step(2)
+    wq_diag()
+    for k in range(3, depth):
+        hid_step(k)
+    advance(2)
+    wq_sib()
+    for slot_id in range(3):
+        ref, dst = ((hidden_ref, hid(t)), (wq_ref.at[z], wq_all.at[mine]), (rest_ref, rest(mine)))[slot_id]
+        pltpu.make_async_copy(ref, dst, own_sems.at[slot_id]).wait()
+    for zz in range(depth):
+        i = 2 * zz + 1 - c
+        arrive(hid(i), hid_sems.at[i])
+
+    rows = wq_all.shape[0] * wq_all.shape[1]
+    for j in range(3):
+        wq_out[:, TYPE * j : TYPE * (j + 1)] = (
+            wq_all[:, :, TYPE * j : TYPE * (j + 1)].astype(F32).reshape(rows, TYPE).astype(BF16)
+        )
+    gain = jnp.transpose(wq_all[:, :, 3 * TYPE :].astype(F32).reshape(rows, LANES))[0:1, :]
+    gain_out[...] = gain
+    advance(1)
+
+    def turn(x, cos, sin):
+        a, d = x[:, :LANES], x[:, LANES:]
+        return jnp.concatenate([a * cos - d * sin, d * cos + a * sin], axis=1)
+
+    def project(p, _):
+        base_row = lax.broadcasted_iota(jnp.int32, (8, LANES), 0)
+        lane8 = lax.broadcasted_iota(jnp.int32, (8, LANES), 1) % half
+        freq8 = jnp.exp(lane8.astype(F32) * (-2.0 / HEAD_DIM * math.log(rope_base)))
+        parts, coss, sins = [], [], []
+        for cc in range(2):
+            blk = 2 * p + cc
+            x = hid_all[blk].astype(F32)
+            centre = jnp.mean(x, axis=-1, keepdims=True)
+            x = x - centre
+            inv = lax.rsqrt(jnp.mean(x * x, axis=-1, keepdims=True) + norm_eps)
+            parts.append((x * inv * gain).astype(BF16))
+            start = (blk * tokens + base_row * 0).astype(F32) * freq8
+            cs, sn = jnp.cos(start)[0:1], jnp.sin(start)[0:1]
+            coss.append(cos_ref[...] * cs - sin_ref[...] * sn)
+            sins.append(sin_ref[...] * cs + cos_ref[...] * sn)
+        h = jnp.concatenate(parts, axis=0)
+        h1_ref[pl.ds(p * 2 * tokens, 2 * tokens), :] = h
+        qkv = jnp.dot(h, wq_out[...], preferred_element_type=F32)
+        cos, sin = jnp.concatenate(coss, axis=0), jnp.concatenate(sins, axis=0)
+        kr = turn(qkv[:, TYPE : 2 * TYPE], cos, sin)
+        k_ref[pl.ds(p * 2 * tokens, 2 * tokens), :] = kr.astype(BF16)
+        v_ref[pl.ds(p * 2 * tokens, 2 * tokens), :] = qkv[:, 2 * TYPE :].astype(BF16)
+        qr = turn(qkv[:, :TYPE], cos, sin).astype(BF16)
+        qr = jnp.where(c == 0, qr[:tokens].astype(F32), qr[tokens:].astype(F32))
+        q_ref[pl.ds(p * tokens, tokens), :] = (qr * HEAD_DIM**-0.5).astype(BF16)
+        return 0
+
+    lax.fori_loop(0, depth, project, 0)
+    advance(2)
+
+    lane_id = lax.broadcasted_iota(jnp.int32, (1, TYPE), 1)
+    lse_lane = lax.broadcasted_iota(jnp.int32, (1, LANES), 1)
+
+    def attend(p, _):
+        at = pl.ds(p * tokens, tokens)
+        q = q_ref[at, :].astype(F32)
+        out = jnp.zeros((tokens, TYPE), F32)
+        lse = jnp.zeros((tokens, LANES), F32)
+        for h in range(heads):
+            rope_mask = ((lane_id % LANES) // half == h).astype(F32)
+            val_mask = (lane_id // HEAD_DIM == h).astype(F32)
+            s = lax.dot_general(
+                (q * rope_mask).astype(BF16),
+                k_ref[...],
+                (((1,), (1,)), ((), ())),
+                preferred_element_type=F32,
+            )
+            peak = jnp.max(s, axis=-1, keepdims=True)
+            e = jnp.exp(s - peak)
+            total = jnp.sum(e, axis=-1, keepdims=True)
+            mix = jnp.dot(e.astype(BF16), v_ref[...], preferred_element_type=F32)
+            out = out + mix * (val_mask / total)
+            lse = lse + (peak + jnp.log(total)) * (lse_lane == h).astype(F32)
+        o_ref[at, :] = out.astype(BF16)
+        att_own[p] = out.astype(BF16)
+        lse_ref[at, :] = lse
+        return 0
+
+    for p in range(depth):
+        attend(p, 0)
+        zz = p
+        sends.go(
+            att_own.at[p],
+            att_ref.at[z],
+            att_sems.at[z],
+            b,
+            2 * zz + c,
+            cond=z != p,
+        )
+        advance(3)
+    advance(len(steps))
+    att_ref[z] = att_own[z]
+    for k in range(1, depth):
+        zz = (z + k) % depth
+        arrive(att_ref.at[zz], att_sems.at[zz])
+    rest_sib()
+    sends.drain()
+
+
+def front(hidden, wq_pack, rest_pack, depth, heads):
+    tokens, width = hidden.shape
+    shards = 8 * depth
+    drows = rest_pack.shape[0]
+    whole = pl.BlockSpec(memory_space=pltpu.VMEM)
+    hbm = pl.BlockSpec(memory_space=pl.ANY)
+    total = 2 * depth * tokens
+    out_shape = (
+        jax.ShapeDtypeStruct((shards,) + rest_pack.shape, BF16),
+        jax.ShapeDtypeStruct((depth, tokens, TYPE), BF16),
+        jax.ShapeDtypeStruct((depth * tokens, TYPE), BF16),
+        jax.ShapeDtypeStruct((total, TYPE), BF16),
+        jax.ShapeDtypeStruct((total, TYPE), BF16),
+        jax.ShapeDtypeStruct((depth * tokens, TYPE), BF16),
+        jax.ShapeDtypeStruct((depth * tokens, LANES), F32),
+        jax.ShapeDtypeStruct((total, width), BF16),
+        jax.ShapeDtypeStruct((shards * drows, 3 * TYPE), BF16),
+        jax.ShapeDtypeStruct((1, width), F32),
+    )
+    return pl.pallas_call(
+        functools.partial(front_kernel, depth, tokens, heads),
+        out_shape=out_shape,
+        in_specs=[whole, whole, hbm],
+        out_specs=[hbm] + [whole] * 9,
+        scratch_shapes=[
+            pltpu.VMEM((2 * depth, tokens, width), BF16),
+            pltpu.VMEM((shards, drows, 3 * TYPE + LANES), BF16),
+            pltpu.VMEM((depth, tokens, TYPE), BF16),
+            pltpu.VMEM((tokens, LANES), F32),
+            pltpu.VMEM((tokens, LANES), F32),
+            pltpu.SemaphoreType.DMA((160,)),
+            pltpu.SemaphoreType.DMA((2 * depth,)),
+            pltpu.SemaphoreType.DMA((shards,)),
+            pltpu.SemaphoreType.DMA((shards,)),
+            pltpu.SemaphoreType.DMA((2, shards)),
+            pltpu.SemaphoreType.DMA((depth,)),
+            pltpu.SemaphoreType.DMA((3,)),
+        ],
+        compiler_params=pltpu.CompilerParams(
+            collective_id=0, has_side_effects=True, vmem_limit_bytes=56 * 2**20
+        ),
+    )(hidden, wq_pack, rest_pack)
+
+
+def pack_heads(w_qkv, depth, heads):
+    half = HEAD_DIM // 2
+    rows = w_qkv.shape[0]
+    used = heads * half
+    pads = ((0, 0), (0, 0), (0, 0), (0, LANES - used))
+    qk = w_qkv[:, : 2 * D].reshape(rows, 2, depth, heads, 2, half)
+    qk = jnp.transpose(qk, (2, 0, 1, 4, 3, 5)).reshape(depth, rows, 4, used)
+    qk = jnp.pad(qk, pads).reshape(depth, rows, 2 * TYPE)
+    v = jnp.transpose(w_qkv[:, 2 * D :].reshape(rows, depth, heads * HEAD_DIM), (1, 0, 2))
+    v = jnp.pad(v, ((0, 0), (0, 0), (0, TYPE - heads * HEAD_DIM)))
+    return jnp.concatenate([qk, v], axis=2)
+
+
+def back_kernel(
+    depth,
+    tokens,
+    heads,
+    splits,
+    datt_ref,
+    q_ref,
+    k_ref,
+    v_ref,
+    o_ref,
+    lse_ref,
+    h1_ref,
+    wq_ref,
+    lt_ref,
+    lt_send,
+    rt_ref,
+    gain2_ref,
+    gain2_send,
+    hidden_ref,
+    gain_ref,
+    dres_ref,
+    rest_out,
+    qkv_out,
+    hid_out,
+    gain_out,
+    dat_all,
+    lt_all,
+    rt_all,
+    gain2_all,
+    grads,
+    hx,
+    hy,
+    fx,
+    fy,
+    ssum,
+    rz,
+    dq_acc,
+    dk_acc,
+    dv_acc,
+    part_own,
+    part_all,
+    dqkv,
+    dh_own,
+    dh_all,
+    qg_wide,
+    qg,
+    qhx,
+    qhy,
+    qfx,
+    qfy,
+    qsum,
+    qz,
+    gain_row,
+    gain_all,
+    send_sems,
+    dat_sems,
+    sib_sems,
+    half_sems,
+    full_sems,
+    z_sems,
+    part_sems,
+    dh_sems,
+    q_sems,
+    qz_sems,
+    gain_sems,
+):
+    b, z, c = place()
+    t = 2 * z + c
+    bx, by = plane_x(b), plane_y(b)
+    bd = plane_x(by)
+    sib = (b, 2 * z + 1 - c)
+    everyone = [
+        ((b + i) % 4, (t + j) % (2 * depth)) for i in range(4) for j in range(2 * depth) if i + j
+    ]
+    greet(everyone)
+    sends = Sends(send_sems)
+    half = HEAD_DIM // 2
+
+    def arrive(dst, sem):
+        remote(dst, dst, send_sems.at[0], sem, *sib).wait_recv()
+
+    def others():
+        return [(z + k) % depth for k in range(1, depth)]
+
+    for j, (src, dst) in enumerate(
+        ((lt_send, lt_all), (rt_ref, rt_all), (gain2_send, gain2_all))
+    ):
+        sends.go(src, dst, sib_sems.at[j], *sib)
+    for zz in others():
+        sends.go(datt_ref.at[zz], dat_all.at[z], dat_sems.at[z], b, 2 * zz + c)
+    dat_all[z] = datt_ref[z]
+
+    for j, (dst,) in enumerate(((lt_all,), (rt_all,), (gain2_all,))):
+        arrive(dst, sib_sems.at[j])
+    rows = lt_ref.shape[1]
+    drows = rows // (4 * depth)
+    step = math.gcd(*splits)
+    col = 0
+    for i, part in enumerate(splits):
+        left = jnp.concatenate([lt_ref[i], lt_all[i]], axis=1)
+        for _ in range(part // step):
+            right = jnp.concatenate(
+                [rt_ref[:, col : col + step], rt_all[:, col : col + step]], axis=0
+            )
+            term = jnp.dot(left, right, preferred_element_type=F32)
+            grads[:, :, col : col + step] = term.reshape(4 * depth, drows, step).astype(BF16)
+            col += step
+    grads[:, :, col:] = (gain2_ref[...].astype(F32) + gain2_all[...].astype(F32)).astype(BF16)
+    width = grads.shape[2]
+    cut = width // 2 // LANES * LANES
+    part_a, part_b = pl.ds(0, cut), pl.ds(cut, width - cut)
+
+    def at(bb, zz):
+        return bb * depth + zz
+
+    def rest_start():
+        for zz in range(depth):
+            sends.go(grads.at[at(bd, zz), :, part_a], hx.at[zz], half_sems.at[0, zz], bx, t)
+            sends.go(grads.at[at(bd, zz), :, part_b], hy.at[zz], half_sems.at[1, zz], by, t)
+
+    def rest_half(zz):
+        arrive(hx.at[zz], half_sems.at[0, zz])
+        i = at(by, zz)
+        grads[i, :, :cut] = (grads[i, :, :cut].astype(F32) + hx[zz].astype(F32)).astype(BF16)
+        sends.go(grads.at[i], fy.at[zz], full_sems.at[1, zz], by, t)
+        arrive(hy.at[zz], half_sems.at[1, zz])
+        i = at(bx, zz)
+        grads[i, :, cut:] = (grads[i, :, cut:].astype(F32) + hy[zz].astype(F32)).astype(BF16)
+        sends.go(grads.at[i], fx.at[zz], full_sems.at[0, zz], bx, t)
+
+    def rest_full(zz):
+        arrive(fx.at[zz], full_sems.at[0, zz])
+        arrive(fy.at[zz], full_sems.at[1, zz])
+        total = grads[at(b, zz)].astype(F32) + fx[zz].astype(F32) + fy[zz].astype(F32)
+
+        @pl.when(z == zz)
+        def _():
+            rest_out[...] = total
+
+        @pl.when(z != zz)
+        def _():
+            ssum[zz] = total.astype(BF16)
+
+        sends.go(ssum.at[zz], rz.at[z], z_sems.at[z], b, 2 * zz + c, cond=z != zz)
+
+    def rest_final():
+        for zz in others():
+            arrive(rz.at[zz], z_sems.at[zz])
+            rest_out[...] += rz[zz].astype(F32)
+
+    steps = []
+    for zz in range(depth + 1):
+        if zz < depth:
+            steps.append(functools.partial(rest_half, zz))
+        if zz > 0:
+            steps.append(functools.partial(rest_full, zz - 1))
+
+    def advance(count):
+        for _ in range(min(count, len(steps))):
+            steps.pop(0)()
+
+    rest_start()
+    for zz in others():
+        arrive(dat_all.at[zz], dat_sems.at[zz])
+
+    lane_id = lax.broadcasted_iota(jnp.int32, (1, TYPE), 1)
+    lse_lane = lax.broadcasted_iota(jnp.int32, (1, LANES), 1)
+    rope_masks = [((lane_id % LANES) // half == h).astype(F32) for h in range(heads)]
+    val_masks = [(lane_id // HEAD_DIM == h).astype(F32) for h in range(heads)]
+    last = (((1,), (1,)), ((), ()))
+    first = (((0,), (0,)), ((), ()))
+
+    def attend(p):
+        rows_p = slice(p * tokens, (p + 1) * tokens)
+        q = q_ref[rows_p, :].astype(F32)
+        da = dat_all[p].astype(F32)
+        mixed = da * o_ref[rows_p, :].astype(F32)
+        lse = lse_ref[rows_p, :]
+        qs = jnp.concatenate([(q * m).astype(BF16) for m in rope_masks], axis=0)
+        das = jnp.concatenate([(da * m).astype(BF16) for m in val_masks], axis=0)
+        delta = jnp.concatenate(
+            [jnp.sum(mixed * m, axis=-1, keepdims=True) for m in val_masks], axis=0
+        )
+        lses = jnp.concatenate(
+            [
+                jnp.sum(lse * (lse_lane == h).astype(F32), axis=-1, keepdims=True)
+                for h in range(heads)
+            ],
+            axis=0,
+        )
+        s = lax.dot_general(qs, k_ref[...], last, preferred_element_type=F32)
+        prob = jnp.exp(s - lses)
+        dp = lax.dot_general(das, v_ref[...], last, preferred_element_type=F32)
+        ds = (prob * (dp - delta)).astype(BF16)
+        low = prob.astype(BF16)
+        dq = jnp.dot(ds, k_ref[...], preferred_element_type=F32)
+        total = dq[:tokens] * rope_masks[0]
+        for h in range(1, heads):
+            total = total + dq[h * tokens : (h + 1) * tokens] * rope_masks[h]
+        dq_acc[rows_p, :] = total * HEAD_DIM**-0.5
+        dk = lax.dot_general(ds, qs, first, preferred_element_type=F32)
+        dv = lax.dot_general(low, das, first, preferred_element_type=F32)
+        if p == 0:
+            dk_acc[...] = dk
+            dv_acc[...] = dv
+        else:
+            dk_acc[...] += dk
+            dv_acc[...] += dv
+
+    for p in range(depth):
+        attend(p)
+        advance(2)
+
+    row = lax.broadcasted_iota(jnp.int32, (tokens, LANES), 0)
+    lane = lax.broadcasted_iota(jnp.int32, (tokens, LANES), 1) % half
+    freq = jnp.exp(lane.astype(F32) * (-2.0 / HEAD_DIM * math.log(rope_base)))
+    base_cos, base_sin = jnp.cos(row.astype(F32) * freq), jnp.sin(row.astype(F32) * freq)
+
+    def unturn(x, blk):
+        start = (blk * tokens + row[:8] * 0).astype(F32) * freq[:8]
+        cs, sn = jnp.cos(start)[0:1], jnp.sin(start)[0:1]
+        cos = base_cos * cs - base_sin * sn
+        sin = base_sin * cs + base_cos * sn
+        a, d = x[:, :LANES], x[:, LANES:]
+        return jnp.concatenate([a * cos + d * sin, d * cos - a * sin], axis=1)
+
+    for blk in range(2 * depth):
+        span = slice(blk * tokens, (blk + 1) * tokens)
+        dk_acc[span, :] = unturn(dk_acc[span, :], blk)
+    part_own[: 2 * depth * tokens, :TYPE] = dk_acc[...].astype(BF16)
+    part_own[: 2 * depth * tokens, TYPE:] = dv_acc[...].astype(BF16)
+    for p in range(depth):
+        span = slice(p * tokens, (p + 1) * tokens)
+        dq_acc[span, :] = unturn(dq_acc[span, :], 2 * p + c)
+    part_q = slice(2 * depth * tokens, 3 * depth * tokens)
+    part_own[part_q, :TYPE] = dq_acc[...].astype(BF16)
+    sends.go(part_own, part_all, part_sems.at[0], *sib)
+    advance(1)
+    arrive(part_all, part_sems.at[0])
+    whole = 2 * depth * tokens
+    dqkv[:, TYPE : 2 * TYPE] = (dk_acc[...] + part_all[:whole, :TYPE].astype(F32)).astype(BF16)
+    dqkv[:, 2 * TYPE :] = (dv_acc[...] + part_all[:whole, TYPE:].astype(F32)).astype(BF16)
+    for p in range(depth):
+        src = slice(whole + p * tokens, whole + (p + 1) * tokens)
+        here = part_own[src, :TYPE].astype(F32)
+        there = part_all[src, :TYPE].astype(F32)
+        even = jnp.where(c == 0, here, there).astype(BF16)
+        odd = jnp.where(c == 0, there, here).astype(BF16)
+        dqkv[2 * p * tokens : (2 * p + 1) * tokens, :TYPE] = even
+        dqkv[(2 * p + 1) * tokens : (2 * p + 2) * tokens, :TYPE] = odd
+
+    for p in range(depth):
+        blk = pl.ds((2 * p + c) * tokens, tokens)
+        dh = lax.dot_general(dqkv[blk, :], wq_ref[...], last, preferred_element_type=F32)
+        dh_own[p] = dh.astype(BF16)
+        sends.go(dh_own.at[p], dh_all.at[z], dh_sems.at[z], b, 2 * p + c, cond=z != p)
+
+    for j in range(3):
+        cols = slice(TYPE * j, TYPE * (j + 1))
+        term = lax.dot_general(h1_ref[...], dqkv[:, cols], first, preferred_element_type=F32)
+        qg_wide[...] = term.reshape(4 * depth, 2, drows, TYPE)
+        qg[:, :, cols] = qg_wide[:, c].astype(BF16)
+    low_z, high_z = pl.ds(0, depth // 2), pl.ds(depth // 2, depth - depth // 2)
+
+    def qrows(bb):
+        return pl.ds(bb * depth, depth)
+
+    def qlow(bb):
+        return pl.ds(bb * depth, depth // 2)
+
+    def qhigh(bb):
+        return pl.ds(bb * depth + depth // 2, depth - depth // 2)
+
+    sends.go(qg.at[qlow(bd)], qhx, q_sems.at[0], bx, t)
+    sends.go(qg.at[qhigh(bd)], qhy, q_sems.at[1], by, t)
+    advance(len(steps))
+    arrive(qhx, q_sems.at[0])
+    qg[qlow(by)] = (qg[qlow(by)].astype(F32) + qhx[...].astype(F32)).astype(BF16)
+    sends.go(qg.at[qrows(by)], qfy, q_sems.at[3], by, t)
+    arrive(qhy, q_sems.at[1])
+    qg[qhigh(bx)] = (qg[qhigh(bx)].astype(F32) + qhy[...].astype(F32)).astype(BF16)
+    sends.go(qg.at[qrows(bx)], qfx, q_sems.at[2], bx, t)
+
+    grad = dh_own[z].astype(F32)
+    for zz in others():
+        arrive(dh_all.at[zz], dh_sems.at[zz])
+        grad = grad + dh_all[zz].astype(F32)
+    x = hidden_ref[...].astype(F32)
+    centre = jnp.mean(x, axis=-1, keepdims=True)
+    x = x - centre
+    inv = lax.rsqrt(jnp.mean(x * x, axis=-1, keepdims=True) + norm_eps)
+    x = x * inv
+    gain_row[...] = jnp.sum(grad * x, axis=0, keepdims=True)
+    me = b * 2 * depth + t
+    for bb, tt in everyone:
+        sends.go(gain_row, gain_all.at[me], gain_sems.at[me], bb, tt)
+    e = grad * gain_ref[...]
+    hid_out[...] = dres_ref[...] + inv * (
+        e - jnp.mean(e, axis=-1, keepdims=True) - x * jnp.mean(e * x, axis=-1, keepdims=True)
+    )
+
+    arrive(qfx, q_sems.at[2])
+    arrive(qfy, q_sems.at[3])
+    total = qg[qrows(b)].astype(F32) + qfx[...].astype(F32) + qfy[...].astype(F32)
+    qsum[...] = total.astype(BF16)
+    for zz in others():
+        sends.go(qsum.at[zz], qz.at[z], qz_sems.at[z], b, 2 * zz + c)
+    qkv_out[z] = qsum[z].astype(F32)
+    rest_final()
+    for zz in others():
+        arrive(qz.at[zz], qz_sems.at[zz])
+        qkv_out[zz] = qz[zz].astype(F32)
+    gains = gain_row[...]
+    for bb, tt in everyone:
+        i = bb * 2 * depth + tt
+        arrive(gain_all.at[i], gain_sems.at[i])
+        gains = gains + gain_all[i]
+    gain_out[...] = gains
+    sends.drain()
+
+
+def back(depth, heads, splits, *operands):
+    tokens, width = operands[13].shape
+    drows = operands[8].shape[1] // (4 * depth)
+    cols = sum(splits) + LANES
+    cut = cols // 2 // LANES * LANES
+    total = 2 * depth * tokens
+    vm = pltpu.VMEM
+    dma = pltpu.SemaphoreType.DMA
+    whole = pl.BlockSpec(memory_space=pltpu.VMEM)
+    blocks = 4 * depth
+    return pl.pallas_call(
+        functools.partial(back_kernel, depth, tokens, heads, splits),
+        out_shape=(
+            jax.ShapeDtypeStruct((drows, cols), F32),
+            jax.ShapeDtypeStruct((depth, drows, 3 * TYPE), F32),
+            jax.ShapeDtypeStruct((tokens, width), F32),
+            jax.ShapeDtypeStruct((1, width), F32),
+        ),
+        in_specs=[whole] * len(operands),
+        out_specs=[whole] * 4,
+        scratch_shapes=[
+            vm((depth, tokens, TYPE), BF16),
+            vm(operands[8].shape, BF16),
+            vm(operands[10].shape, BF16),
+            vm(operands[11].shape, BF16),
+            vm((blocks, drows, cols), BF16),
+            vm((depth, drows, cut), BF16),
+            vm((depth, drows, cols - cut), BF16),
+            vm((depth, drows, cols), BF16),
+            vm((depth, drows, cols), BF16),
+            vm((depth, drows, cols), BF16),
+            vm((depth, drows, cols), BF16),
+            vm((depth * tokens, TYPE), F32),
+            vm((total, TYPE), F32),
+            vm((total, TYPE), F32),
+            vm((3 * depth * tokens, 2 * TYPE), BF16),
+            vm((3 * depth * tokens, 2 * TYPE), BF16),
+            vm((total, 3 * TYPE), BF16),
+            vm((depth, tokens, width), BF16),
+            vm((depth, tokens, width), BF16),
+            vm((blocks, 2, drows, TYPE), F32),
+            vm((blocks, drows, 3 * TYPE), BF16),
+            vm((depth // 2, drows, 3 * TYPE), BF16),
+            vm((depth - depth // 2, drows, 3 * TYPE), BF16),
+            vm((depth, drows, 3 * TYPE), BF16),
+            vm((depth, drows, 3 * TYPE), BF16),
+            vm((depth, drows, 3 * TYPE), BF16),
+            vm((depth, drows, 3 * TYPE), BF16),
+            vm((1, width), F32),
+            vm((8 * depth, 1, width), F32),
+            dma((96,)),
+            dma((depth,)),
+            dma((3,)),
+            dma((2, depth)),
+            dma((2, depth)),
+            dma((depth,)),
+            dma((1,)),
+            dma((depth,)),
+            dma((4,)),
+            dma((depth,)),
+            dma((8 * depth,)),
+        ],
+        compiler_params=pltpu.CompilerParams(
+            collective_id=1, has_side_effects=True, vmem_limit_bytes=60 * 2**20
+        ),
+    )(*operands)
+
+
+def unpack_heads(grad, depth, heads):
+    half = HEAD_DIM // 2
+    rows = grad.shape[1]
+    qk = grad[:, :, : 2 * TYPE].reshape(depth, rows, 2, 2, LANES)[..., : heads * half]
+    qk = qk.reshape(depth, rows, 2, 2, heads, half)
+    qk = jnp.transpose(qk, (1, 2, 0, 4, 3, 5)).reshape(rows, 2 * D)
+    v = jnp.transpose(grad[:, :, 2 * TYPE : 2 * TYPE + heads * HEAD_DIM], (1, 0, 2))
+    return jnp.concatenate([qk, v.reshape(rows, D)], axis=1)
+
+
+def by_heads(
+    depth, heads, hidden, cotangent, w_qkv, w_proj, w_inner, w_down, norm1_gain, norm2_gain
+):
+    tokens = hidden.shape[1]
+    rows = w_qkv.shape[0]
+    core = lax.axis_index("ctx") % 2
+    column = lambda gain: jnp.pad(gain[:, None], ((0, 0), (0, LANES - 1)))
+    gain_block = jnp.broadcast_to(column(norm1_gain)[None], (depth, rows, LANES))
+    wq_pack = jnp.concatenate([pack_heads(w_qkv, depth, heads), gain_block], axis=2)
+    rest_pack = jnp.concatenate([w_proj, w_inner, w_down, column(norm2_gain)], axis=1)
+    rest_all, att, q, k, v, o, lse, h1, wq, first_gain = front(
+        hidden[0], wq_pack, rest_pack, depth, heads
+    )
+    rest_all = rest_all.reshape(D, rest_pack.shape[1])
+    splits = (w_proj.shape[1], w_inner.shape[1], w_down.shape[1])
+    edges = [0]
+    for part in splits:
+        edges.append(edges[-1] + part)
+    full_proj, full_inner, full_down = (rest_all[:, edges[i] : edges[i + 1]] for i in range(3))
+    second_norm_gain = rest_all[:, edges[3]].astype(F32)
+    used = heads * HEAD_DIM
+    attended = jnp.transpose(att[:, :, :used], (1, 0, 2)).reshape(tokens, D)
+    residual_stream = hidden[0].astype(F32) + jnp.dot(
+        attended, full_proj, preferred_element_type=F32
+    )
+    second_normed_rows, second_centered_rows, second_inverse_deviation = apply_layer_norm(
+        residual_stream, second_norm_gain
+    )
+    h_two = second_normed_rows.astype(BF16)
+    inner_all = jnp.dot(h_two, full_inner, preferred_element_type=F32)
+    act_half = inner_all[:, :FF]
+    gate_half = inner_all[:, FF:]
+    activated, gelu_slope = gelu_parts(act_half)
+    middle = (activated * gate_half).astype(BF16)
+    output_rows = residual_stream + jnp.einsum(
+        "tf,df->td", middle, full_down, preferred_element_type=F32
+    )
+    upstream = cotangent[0]
+    d_middle = jnp.dot(upstream, full_down, preferred_element_type=F32)
+    d_inner = jnp.concatenate(
+        [d_middle * gate_half * gelu_slope, d_middle * activated], axis=-1
+    ).astype(BF16)
+    second_hidden_gradient = jnp.einsum(
+        "te,de->td", d_inner, full_inner, preferred_element_type=F32
+    )
+    residual_norm_gradient, second_gain_portion = layer_norm_gradient(
+        second_hidden_gradient, second_norm_gain, second_centered_rows, second_inverse_deviation
+    )
+    d_resid = upstream.astype(F32) + residual_norm_gradient
+    d_resid_low = d_resid.astype(BF16)
+    d_attended = jnp.einsum(
+        "td,ed->te", d_resid_low, full_proj, preferred_element_type=F32
+    ).astype(BF16)
+    datt = jnp.pad(
+        jnp.transpose(d_attended.reshape(tokens, depth, used), (1, 0, 2)),
+        ((0, 0), (0, 0), (0, TYPE - used)),
+    )
+    lefts = jnp.stack([jnp.transpose(a) for a in (attended, h_two, upstream)])
+    lefts = lefts.reshape(3, 4 * depth, 2, rows, tokens)
+    gains = jnp.pad(second_gain_portion[:, None], ((0, 0), (0, LANES - 1))).astype(BF16)
+    gains = gains.reshape(4 * depth, 2, rows, LANES)
+
+    def lane_of(array, axis, which):
+        return lax.dynamic_index_in_dim(array, which, axis, keepdims=False)
+
+    def left_of(which):
+        return lane_of(lefts, 2, which).reshape(3, 4 * depth * rows, tokens)
+
+    rights = jnp.concatenate([d_resid_low, d_inner, middle], axis=1)
+    rest_grad, qkv_grad, hidden_grad, gain_total = back(
+        depth,
+        heads,
+        splits,
+        datt,
+        q,
+        k,
+        v,
+        o,
+        lse,
+        h1,
+        wq,
+        left_of(core),
+        left_of(1 - core),
+        rights,
+        lane_of(gains, 1, core),
+        lane_of(gains, 1, 1 - core),
+        hidden[0],
+        first_gain,
+        d_resid,
+    )
+    own = (lax.axis_index("batch") * 2 * depth + lax.axis_index("ctx")) * rows
+    return (
+        output_rows.astype(BF16)[None],
+        hidden_grad[None],
+        unpack_heads(qkv_grad, depth, heads),
+        rest_grad[:, edges[0] : edges[1]],
+        rest_grad[:, edges[1] : edges[2]],
+        rest_grad[:, edges[2] : edges[3]],
+        lax.dynamic_slice_in_dim(gain_total[0], own, rows),
+        rest_grad[:, edges[3]],
+    )
+
+
 def solution(mesh):
     placed = (
         P("batch", "ctx", None),
@@ -294,8 +1227,14 @@
         P(("batch", "ctx")),
         P(("batch", "ctx")),
     )
+    width = mesh.shape["ctx"]
+    depth = width // 2
+    heads = HEADS // max(depth, 1)
+    plane = mesh.shape["batch"] == 4 and width == 2 * depth and depth % 2 == 0
+    fits = heads * depth == HEADS and heads * HEAD_DIM <= TYPE and heads * HEAD_DIM <= 2 * LANES
+    body = functools.partial(by_heads, depth, heads) if plane and fits else local
     return jax.shard_map(
-        local,
+        body,
         mesh=mesh,
         in_specs=placed,
         out_specs=(

time: 394 us -> 183 us (0.46)
  waiting for transfers between devices: 288 us -> 0 us
  Pallas kernels: 14.5 us -> 149 us
  matrix products: 28.4 us -> 11.4 us
  between operations: 14.4 us -> 0.98 us
  other arithmetic: 17.7 us -> 4.69 us
  local copies, waits for them, and re-layouts: 29.3 us -> 17 us
    reduce_scatter x2 -> x0, waiting for transfers between devices: 166 us -> none  [the longest x1 135 us: local(): lax.psum_scatter(grad_terms, EVERY, scatter_dimension=0, tiled=True)]
    pallas_call x1 -> x2, Pallas kernels: 14.5 us -> 149 us  [the longest x1 82.2 us: back(): pl.pallas_call(functools.partial(back_kernel, depth, tokens, heads, split...]
    all_gather x2 -> x0, waiting for transfers between devices: 122 us -> none  [the longest x1 84.9 us: local(): lax.all_gather(jnp.concatenate([w_qkv, w_proj, w_inner, w_down, gains], a...]
    dot_general x14 -> x6, matrix products: 28.4 us -> 11.4 us  [the longest x1 2.83 us: by_heads(): inner_all = jnp.dot(h_two, full_inner, preferred_element_type=F32)]
    unnamed x85 -> x25, local copies, waits for them, and re-layouts: 9.97 us -> 1.71 us
    slice x11 -> x8, local copies, waits for them, and re-layouts: 12 us -> 6.23 us  [the longest x1 0.95 us: by_heads(): second_norm_gain = rest_all[:, edges[3]].astype(F32)]
    convert_element_type x7 -> x1, local copies, waits for them, and re-layouts: 4.91 us -> 0.16 us  [by_heads(): d_attended = jnp.einsum('td,ed->te', d_resid_low, full_proj, preferred_el...]
    convert_element_type x6 -> x2, other arithmetic: 5.07 us -> 0.99 us  [the longest x1 0.95 us: by_heads(): d_resid_low = d_resid.astype(BF16)]
  transfers between devices with their start and end apart: 4 -> 0, of which waited for: 4 -> 0; matrix products, arithmetic and copies ran while one was open for 4% -> 0% of each run, Pallas kernels for 0% -> 0%
where the time goes in v1:
time: 183 us
  Pallas kernels  149 us (81%)
  local copies, waits for them, and re-layouts  17 us (9%)
  matrix products  11.4 us (6%)
  other arithmetic  4.69 us (3%)
    pallas_call x1, Pallas kernels, back(): pl.pallas_call(functools.partial(back_kernel, depth, tokens, heads, split...  82.2 us
    pallas_call x1, Pallas kernels, front(): pl.pallas_call(functools.partial(front_kernel, depth, tokens, heads), out...  66.4 us

profile of v1, /device:TPU:0, one launch (start us, length us, event | category | flops | bytes accessed | tf_op | source)
XLA Modules:
  0.0 182.8 jit_solution(7086831239798866131)
XLA Ops:
  0.7 0.8 slice.49
  1.6 0.7 copy.58
  2.4 0.9 slice.48
  3.9 0.7 fusion.33.wq_ref
  4.7 0.7 fusion.30.rest_ref
  5.4 66.4 %shard_map.143 = (bf16[32,24,4352]{2,1,0:T(8,128)(2,1)}, bf16[4,128,256]{2,1,0:T(8,128)(2,1)}, bf16[512,256]{1,0:T(8,128)(2,1)}, bf16[1024,256]{1,0:T(8,128)(2,1...) custom-call(bf16[128,768]{1,0:T(8,128)(2,1)} %bitcast.72, ...), custom_call_target="tpu_custom_call" | custom-call | tf_op jit(solution)/shard_map/pallas_call | solution.py:679
  71.9 1.0 slice_bitcast_fusion
  73.0 1.7 fusion.38
  74.8 0.9 slice.65
  76.1 2.8 %fusion.2 = f32[128,2304]{1,0:T(8,128)S(1)} fusion(bf16[768,4352]{1,0:T(8,128)(2,1)} %bitcast.62, f32[128,768]{1,0:T(8,128)S(1)} %get-tuple-element.50, f32[768]{0:T(1024)S(1)} %convert_reduce_fusion, f32[128]{0:T(128)S(1)} %add_rsqrt_fusion, f32[128]{0:T(128)S(1)} %broadcast_multiply_fusion.2), kind=kOutput, calls=%fused_computation.2 | convolution fusion | flops 453378048 | bytes 5115904 | tf_op jit(solution)/shard_map/dot_general | solution.py:1145
  79.0 2.3 %fusion.23 = (bf16[128,1152]{1,0:T(8,128)(2,1)S(1)}, bf16[128,1152]{1,0:T(8,128)(2,1)S(1)}, bf16[128,1152]{1,0:T(8,128)(2,1)S(1)}) fusion(f32[128,2304]{1,0:T(8,128)S(1)} %fusion.2, bf16[768,4352]{1,0:T(8,128)(2,1)} %bitcast.63, bf16[1,128,768]{2,1,0:T(8,128)(2,1)S(1)} %copy-done.1), kind=kOutput, calls=%fused_computation.22 | convolution fusion | flops 228851712 | bytes 4030464 | tf_op jit(solution)/shard_map/dot_general | solution.py:1154
  81.2 2.8 %fusion.13 = bf16[1,128,768]{2,1,0:T(8,128)(2,1)} fusion(f32[128,768]{1,0:T(8,128)S(1)} %get-tuple-element.50, bf16[128,1152]{1,0:T(8,128)(2,1)S(1)} %get-tuple-element.43, bf16[768,4352]{1,0:T(8,128)(2,1)} %bitcast.64), kind=kOutput, calls=%fused_computation.12 | convolution fusion | flops 226689024 | bytes 2654208 | tf_op jit(solution)/shard_map/tf,df->td/dot_general | solution.py:1150
  84.0 1.3 fusion
  85.6 0.9 fusion.37
  86.6 0.5 convolution_convert_fusion
  87.4 0.7 pad.28.datt_ref
  88.6 0.9 constant_dynamic-slice_fusion.1
  89.5 1.1 pad_maximum_fusion.rt_ref
  90.8 0.7 dynamic-slice_bitcast_fusion
  91.5 82.2 %shard_map.144 = (f32[24,4352]{1,0:T(8,128)}, f32[4,24,768]{2,1,0:T(8,128)}, f32[128,768]{1,0:T(8,128)}, f32[1,768]{1,0:T(1,128)}) custom-call(bf16[4,128,256]{2,1,0:T(8,128)(2,1)} %pad.28.datt_ref, bf16[512,256]{1,0:T(8,128)(2,1)} %get-tuple-element.24.q_ref, bf16[1024,256]{1,0:T(8,128)(2,1)} %get-tuple-element.25.k_ref, ...), custom_call_target="tpu_custom_call" | custom-call | tf_op jit(solution)/shard_map/pallas_call | solution.py:1048
  173.7 0.9 slice_bitcast_fusion.1
  174.8 0.9 slice.57
  175.9 0.3 reshape.107
  176.2 0.5 copy.52
  176.7 0.8 reshape.108
  177.5 0.7 pad_maximum_fusion.2
  178.2 0.6 slice.60
  178.8 0.7 slice.61
  179.5 0.7 slice.62
  180.2 1.2 fusion.34
  181.5 0.6 slice_reduce_fusion
  182.1 0.7 copy.65
  (51 shorter events, 2.9 us)
Async XLA Ops:
  0.6 4.0 %copy-start.7 = (bf16[24]{0:T(256)(128)(2,1)S(1)}, bf16[24]{0:T(256)(128)(2,1)}, u32[]{:S(2)}) copy-start(bf16[24]{0:T(256)(128)(2,1)} %param.15) | copy-start | bytes 148
  0.6 4.1 %copy-start.5 = (bf16[24,1152]{1,0:T(8,128)(2,1)S(1)}, bf16[24,1152]{1,0:T(8,128)(2,1)}, u32[]{:S(2)}) copy-start(bf16[24,1152]{1,0:T(8,128)(2,1)} %param.13) | copy-start | bytes 165892
  0.7 4.1 %copy-start.4 = (bf16[24,2304]{1,0:T(8,128)(2,1)S(1)}, bf16[24,2304]{1,0:T(8,128)(2,1)}, u32[]{:S(2)}) copy-start(bf16[24,2304]{1,0:T(8,128)(2,1)} %param.12) | copy-start | bytes 331780
  0.7 4.1 %copy-start.6 = (bf16[24,768]{1,0:T(8,128)(2,1)S(1)}, bf16[24,768]{1,0:T(8,128)(2,1)}, u32[]{:S(2)}) copy-start(bf16[24,768]{1,0:T(8,128)(2,1)} %param.11) | copy-start | bytes 110596
  3.3 69.7 %copy-start = (bf16[1,128,768]{2,1,0:T(8,128)(2,1)S(1)}, bf16[1,128,768]{2,1,0:T(8,128)(2,1)}, u32[]{:S(2)}) copy-start(bf16[1,128,768]{2,1,0:T(8,128)(2,1)} %param.8) | copy-start | bytes 589828
  76.1 2.9 %copy-start.1 = (bf16[1,128,768]{2,1,0:T(8,128)(2,1)S(1)}, bf16[1,128,768]{2,1,0:T(8,128)(2,1)}, u32[]{:S(2)}) copy-start(bf16[1,128,768]{2,1,0:T(8,128)(2,1)} %param.9) | copy-start | bytes 589828
  76.1 7.9 %slice-start = ((s8[6684672]{0:T(1024)(128)(4,1)}), s8[4194304]{0:T(1024)(128)(4,1)S(1)}, s32[]{:S(2)}) async-start(s8[6684672]{0:T(1024)(128)(4,1)} %bitcast.65), calls=%async_computation | async-start | bytes 8388608
  78.9 5.1 %slice-start.1 = ((s8[6684672]{0:T(1024)(128)(4,1)}), s8[2490368]{0:T(1024)(128)(4,1)S(1)}, s32[]{:S(2)}) async-start(s8[6684672]{0:T(1024)(128)(4,1)} %bitcast.65), calls=%async_computation.1 | async-start | bytes 4980736
  175.7 2.5 %copy-start.2 = (f32[24,4352]{1,0:T(8,128)S(1)}, f32[24,4352]{1,0:T(8,128)}, u32[]{:S(2)}) copy-start(f32[24,4352]{1,0:T(8,128)} %get-tuple-element.34) | copy-start | bytes 1253380
  175.9 6.2 %copy-start.3 = (f32[128,768]{1,0:T(8,128)S(1)}, f32[128,768]{1,0:T(8,128)}, u32[]{:S(2)}) copy-start(f32[128,768]{1,0:T(8,128)} %get-tuple-element.32) | copy-start | bytes 1179652
